TPU v7x, 32 devices: a whole 2x2x4 slice. The times are simulated.
32 devices in a mesh: grp: 2 (over y), scen: 4 (over z), blk: 2 (over x), sub: 2 (over core).
Axes of the slice: x: 2, y: 2, z: 4, core: 2. Of those that a mesh axis runs over, the one named last changes fastest.
Arguments:
- block_matrices: float32 [8, 256, 128, 128], P(('grp', 'scen'), ('blk', 'sub')), parts along dimension 0, may hold values from -0.25 to 0.25
- slot_row_block: int32 [8, 256], P(('grp', 'scen'), ('blk', 'sub')), parts along dimension 0, may hold values from 0 to 7
- tile_column: int32 [8, 256], P(('grp', 'scen'), ('blk', 'sub')), parts along dimension 0, may hold values from 0 to 4127, as said below
- block_count: int32 [8, 4], P(('grp', 'scen'), ('blk', 'sub')), parts along dimension 0, may hold values from 8 to 64, as said below
- carbon_scenario: int32 [8], P(('grp', 'scen')), parts along dimension 0, may hold values from 0 to 23
- intensity: float32 [24, 32, 128], P(None, ('blk', 'sub')), may hold values from 0.2 to 2
- cost_first: float32 [8192, 128], P(('grp', 'scen', 'blk', 'sub')), parts along dimension 0, may hold values from -6 to 6
- lower_first: float32 [8192, 128], P(('grp', 'scen', 'blk', 'sub')), parts along dimension 0, may hold values from -1 to -0.2
- upper_first: float32 [8192, 128], P(('grp', 'scen', 'blk', 'sub')), parts along dimension 0, may hold values from 0.2 to 1
- cost_second: float32 [8, 32, 128], P(('grp', 'scen'), ('blk', 'sub')), parts along dimension 0, may hold values from -6 to 6
- upper_second: float32 [8, 32, 128], P(('grp', 'scen'), ('blk', 'sub')), parts along dimension 0, may hold values from 0.2 to 2
- row_bound: float32 [8, 32, 128], P(('grp', 'scen'), ('blk', 'sub')), parts along dimension 0, may hold values from -20 to 20
- first_start: float32 [8192, 128], P(('grp', 'scen', 'blk', 'sub')), parts along dimension 0, may hold values from -0.2 to 0.2
- second_start: float32 [8, 32, 128], P(('grp', 'scen'), ('blk', 'sub')), parts along dimension 0, may hold values from 0 to 0.2
- dual_start: float32 [8, 32, 128], P(('grp', 'scen'), ('blk', 'sub')), parts along dimension 0, may hold values from 0 to 1
Outputs:
- first_final: float32 [8192, 128], P(('grp', 'scen', 'blk', 'sub')), parts along dimension 0
- second_final: float32 [8, 32, 128], P(('grp', 'scen'), ('blk', 'sub')), parts along dimension 0
- dual_final: float32 [8, 32, 128], P(('grp', 'scen'), ('blk', 'sub')), parts along dimension 0
- residual_norm: float32 [6], P('grp'), parts along dimension 0
There are 2 independent parts, one for each index of `grp`. A program takes and returns all parts, laid end to end along the dimension named above; an argument that names none is the same for every part. Nothing has to cross between parts.
Inputs may be any that keep to these rules, and one draw needn't show every extreme that they name: `block_count`: each scenario has one index of blk and sub with all 64 slots used; the others use between 8 and 32. `tile_column`: values below 4096 name first-section column blocks, values from 4096 on second-section ones. Split the first-section blocks into 16 equal shards in order, and take the slots of one index of scen and of blk and sub together (64 of them, scenario by scenario). In every draw, on every such device, at most 4 of them name first-section blocks of one shard, and some shard is named by exactly 4.
All inputs are finite; a program needn't handle non-finite values.
Results may differ from a plain program's by a relative error of at most 0.0003.
Values sent between devices are 32-bit elements; how exact they have to be, the bound alone decides.
No kernel may reach another device: no remote copies, remote signals or barrier semaphores. Data moves between devices by JAX's collectives and lax.ppermute only.
A program may use at most 64 MiB of HBM per device.

v0:
```python
import jax
import jax.numpy as jnp
from jax import lax
from jax.sharding import PartitionSpec as P

ITERS = 3
precise = lax.Precision.HIGHEST
step_primal = 0.4
step_dual = 0.4


def forward_window(
    block_matrices,
    onehot,
    mask,
    tile_column,
    fetch_first,
    count_first,
    second_bar,
    offset,
    window_size,
):
    count_second = second_bar.shape[1]
    is_first = tile_column < count_first
    from_first = fetch_first(tile_column, offset, window_size)
    second_index = jnp.clip(tile_column - count_first, 0, count_second - 1)
    from_second = jax.vmap(lambda table, index: table[index])(second_bar, second_index)
    blocks = jnp.where(is_first[:, :, None], from_first, from_second)
    product = jnp.einsum("skij,skj->ski", block_matrices, blocks, precision=precise)
    product = product * mask[:, :, None]
    return jnp.einsum("skr,ski->sri", onehot, product, precision=precise)


def adjoint_window(
    block_matrices,
    onehot,
    mask,
    tile_column,
    dual,
    collect_first,
    count_first,
    count_second,
    offset,
    window_size,
):
    gathered = jnp.einsum("skr,sri->ski", onehot, dual, precision=precise)
    product = jnp.einsum("skij,ski->skj", block_matrices, gathered, precision=precise)
    product = product * mask[:, :, None]
    is_first = tile_column < count_first
    first_terms = collect_first(product, tile_column, offset, window_size)
    second_index = jnp.where(is_first, count_second, tile_column - count_first)
    scenario_index = lax.broadcasted_iota(jnp.int32, second_index.shape, 0)
    second_terms = (
        jnp.zeros((product.shape[0], count_second, product.shape[2]), jnp.float32)
        .at[scenario_index, second_index]
        .add(product, mode="drop")
    )
    return (first_terms, second_terms)


def shards(
    block_matrices,
    slot_row_block,
    tile_column,
    block_count,
    carbon_scenario,
    intensity,
    cost_first,
    lower_first,
    upper_first,
    cost_second,
    upper_second,
    row_bound,
    first_start,
    second_start,
    dual_start,
):
    scen_local, slots = slot_row_block.shape
    rows_local = row_bound.shape[1]
    tile_size = row_bound.shape[2]
    shard_first = cost_first.shape[0]
    owner_count = lax.axis_size(("scen", "blk", "sub"))
    count_first = shard_first * owner_count
    count_second = cost_second.shape[1] * lax.axis_size(("blk", "sub"))
    total_cells = scen_local * rows_local * tile_size * owner_count
    mask = (jnp.arange(slots, dtype=jnp.int32)[None, :] < block_count).astype(jnp.float32)
    onehot = (
        slot_row_block[:, :, None] == jnp.arange(rows_local, dtype=jnp.int32)[None, None, :]
    ).astype(jnp.float32)
    choose = (
        carbon_scenario[:, None] == jnp.arange(intensity.shape[0], dtype=jnp.int32)[None, :]
    ).astype(jnp.float32)
    cost_total = cost_second + jnp.einsum("sc,cbt->sbt", choose, intensity, precision=precise)
    first_shape = (count_first, tile_size)

    def collect_first(product, column_window, offset, width):
        first_index = jnp.where(column_window < count_first, column_window, count_first).reshape(-1)
        return (
            jnp.zeros(first_shape, jnp.float32)
            .at[first_index]
            .add(product.reshape(-1, tile_size), mode="drop")
        )

    def make_fetch(first_source):

        def fetch_first(column_window, offset, width):
            return first_source[jnp.clip(column_window, 0, count_first - 1)]

        return fetch_first

    cost_all, lower_all, upper_all, first_now = (
        lax.all_gather(cost_first, ("scen", "blk", "sub"), axis=0, tiled=True),
        lax.all_gather(lower_first, ("scen", "blk", "sub"), axis=0, tiled=True),
        lax.all_gather(upper_first, ("scen", "blk", "sub"), axis=0, tiled=True),
        lax.all_gather(first_start, ("scen", "blk", "sub"), axis=0, tiled=True),
    )
    second_now = second_start
    dual = dual_start
    squares = []
    for step_index in range(ITERS):
        grad_first_part, grad_second_part = adjoint_window(
            block_matrices,
            onehot,
            mask,
            tile_column,
            dual,
            collect_first,
            count_first,
            count_second,
            0,
            slots,
        )
        grad_second = lax.psum_scatter(
            grad_second_part, ("blk", "sub"), scatter_dimension=1, tiled=True
        )
        grad_first = lax.psum(grad_first_part, ("scen", "blk", "sub"))
        first_next = jnp.clip(
            first_now - step_primal * (cost_all - grad_first), lower_all, upper_all
        )
        first_source = 2.0 * first_next - first_now
        second_next = jnp.clip(
            second_now - step_primal * (cost_total - grad_second), 0.0, upper_second
        )
        second_bar = lax.all_gather(
            2.0 * second_next - second_now, ("blk", "sub"), axis=1, tiled=True
        )
        residual = row_bound - forward_window(
            block_matrices,
            onehot,
            mask,
            tile_column,
            make_fetch(first_source),
            count_first,
            second_bar,
            0,
            slots,
        )
        local_square = jnp.sum(residual * residual)
        squares.append(lax.psum(local_square, ("scen", "blk", "sub")))
        dual = jnp.maximum(dual + step_dual * residual, 0.0)
        first_now = first_next
        second_now = second_next
    totals = jnp.stack(squares)
    residual_norm = jnp.sqrt(totals / total_cells)
    offset = lax.axis_index(("scen", "blk", "sub")) * shard_first
    first_final = lax.dynamic_slice_in_dim(first_now, offset, shard_first, 0)
    return (first_final, second_now, dual, residual_norm)


def solution(mesh):
    return jax.shard_map(
        shards,
        mesh=mesh,
        in_specs=(
            P(("grp", "scen"), ("blk", "sub"), None, None),
            P(("grp", "scen"), ("blk", "sub")),
            P(("grp", "scen"), ("blk", "sub")),
            P(("grp", "scen"), ("blk", "sub")),
            P(("grp", "scen")),
            P(None, ("blk", "sub"), None),
            P(("grp", "scen", "blk", "sub"), None),
            P(("grp", "scen", "blk", "sub"), None),
            P(("grp", "scen", "blk", "sub"), None),
            P(("grp", "scen"), ("blk", "sub"), None),
            P(("grp", "scen"), ("blk", "sub"), None),
            P(("grp", "scen"), ("blk", "sub"), None),
            P(("grp", "scen", "blk", "sub"), None),
            P(("grp", "scen"), ("blk", "sub"), None),
            P(("grp", "scen"), ("blk", "sub"), None),
        ),
        out_specs=(
            P(("grp", "scen", "blk", "sub"), None),
            P(("grp", "scen"), ("blk", "sub"), None),
            P(("grp", "scen"), ("blk", "sub"), None),
            P("grp"),
        ),
        check_vma=False,
    )
```

profile of v0, /device:TPU:0, one launch (start us, length us, event | category | flops | bytes accessed | tf_op | source)
XLA Modules:
  0.0 587.6 jit_solution(10443737884723280404)
XLA Ops:
  7.2 0.0 all-reduce.9.cloned.1.call-start
  7.9 0.7 fusion.79
  8.5 0.9 fusion.66
  9.5 5.3 fusion.10
  14.8 2.3 scatter_custom_fusion
  17.1 0.0 all-reduce.9.cloned.1.call-update
  17.1 0.0 all-gather.11.cloned.1.call-start
  17.2 0.7 all-gather.11.cloned.1.call-update
  17.9 0.0 all-gather.5.cloned.1.call-start
  17.9 0.7 all-gather.5.cloned.1.call-update
  18.6 0.0 all-gather.7.cloned.1.call-start
  18.7 0.5 all-gather.7.cloned.1.call-update
  19.2 0.0 all-gather.9.cloned.1.call-start
  19.2 0.5 all-gather.9.cloned.1.call-update
  19.8 0.0 all-reduce.11.cloned.1.call-start
  19.9 0.9 scatter_custom_fusion.1
  21.4 0.6 dynamic-slice
  22.7 13.2 %all-reduce.1 = f32[1,32,128]{2,1,0:T(8,128)S(1)} all-reduce(f32[1,32,128]{2,1,0:T(8,128)S(1)} %bitcast.135), channel_id=2, replica_groups=mesh['grp'=2,'scen'=4,'blk'=2,'sub'=2] {'blk','sub'}, use_global_device_ids=true, to_apply=%region_3.4.clone | all-reduce | flops 4096 | bytes 32768
  35.8 0.2 fusion.21
  36.1 5.2 all_gather.25
  41.3 0.8 gather_fusion.3
  42.1 75.8 %all-reduce.9.cloned.1.call-done = f32[4096,128]{1,0:T(8,128)} async-done(((f32[4096,128]{1,0:T(8,128)}), f32[4096,128]{1,0:T(8,128)}) %all-reduce.9.cloned.1.call-update) | async-done | bytes 2097168 | tf_op jit(solution)/shard_map/psum | solution.py:136
  117.9 43.1 %all-gather.11.cloned.1.call-done = f32[4096,128]{1,0:T(8,128)} async-done(((f32[256,128]{1,0:T(8,128)}), f32[4096,128]{1,0:T(8,128)}) %all-gather.11.cloned.1.call-update) | async-done | bytes 2097168 | tf_op jit(solution)/shard_map/all_gather | solution.py:112
  160.9 42.6 %all-gather.5.cloned.1.call-done = f32[4096,128]{1,0:T(8,128)} async-done(((f32[256,128]{1,0:T(8,128)}), f32[4096,128]{1,0:T(8,128)}) %all-gather.5.cloned.1.call-update) | async-done | bytes 2097168 | tf_op jit(solution)/shard_map/all_gather | solution.py:114
  203.6 42.5 %all-gather.7.cloned.1.call-done = f32[4096,128]{1,0:T(8,128)} async-done(((f32[256,128]{1,0:T(8,128)}), f32[4096,128]{1,0:T(8,128)}) %all-gather.7.cloned.1.call-update) | async-done | bytes 2097168 | tf_op jit(solution)/shard_map/all_gather | solution.py:113
  246.0 42.4 %all-gather.9.cloned.1.call-done = f32[4096,128]{1,0:T(8,128)} async-done(((f32[256,128]{1,0:T(8,128)}), f32[4096,128]{1,0:T(8,128)}) %all-gather.9.cloned.1.call-update) | async-done | bytes 2097168 | tf_op jit(solution)/shard_map/all_gather | solution.py:115
  288.5 5.9 %multiply_subtract_fusion.2 = (f32[4096,128]{1,0:T(8,128)S(1)}, f32[4096,128]{1,0:T(8,128)}) fusion(f32[4096,128]{1,0:T(8,128)} %all-gather.9.cloned.1.call-done, f32[4096,128]{1,0:T(8,128)} %all-gather.5.cloned.1.call-done, f32[4096,128]{1,0:T(8,128)} %all-gather.7.cloned.1.call-done, f32[4096,128]{1,0:T(8,128)} %all-gather.11.cloned.1.call-done, ...), kind=kLoop, calls=%fused_computation.28 | loop fusion | flops 3670016 | bytes 14680064 | tf_op jit(solution)/shard_map/sub | solution.py:140
  294.4 0.6 gather_fusion
  295.0 0.1 broadcast_select_fusion.2
  295.1 8.5 %fusion.8 = f32[64,1,128]{2,1,0:T(1,128)S(1)} fusion(f32[64,128,1]{1,2,0:T(1,128)S(1)} %bitcast.130, f32[1,64,128,128]{3,2,1,0:T(8,128)} %param.15), kind=kOutput, calls=%fused_computation.20 | convolution fusion | flops 12582912 | bytes 4259840 | tf_op jit(solution)/shard_map/skij,skj->ski/dot_general | solution.py:29
  303.6 0.3 fusion.14
  303.8 0.2 fusion.64
  304.1 3.7 fusion.6
  307.7 2.3 scatter_custom_fusion.2
  310.0 0.0 all-reduce.11.cloned.1.call-update
  310.0 0.0 all-reduce.13.cloned.1.call-start
  310.1 0.9 scatter_custom_fusion.3
  311.0 10.4 %all-reduce.2 = f32[1,32,128]{2,1,0:T(8,128)S(1)} all-reduce(f32[1,32,128]{2,1,0:T(8,128)S(1)} %bitcast.137), channel_id=3, replica_groups=mesh['grp'=2,'scen'=4,'blk'=2,'sub'=2] {'blk','sub'}, use_global_device_ids=true, to_apply=%region_7.8.clone | all-reduce | flops 4096 | bytes 32768
  321.4 5.4 all_gather.26
  326.7 0.8 gather_fusion.4
  327.5 79.2 %all-reduce.11.cloned.1.call-done = f32[4096,128]{1,0:T(8,128)} async-done(((f32[4096,128]{1,0:T(8,128)}), f32[4096,128]{1,0:T(8,128)}) %all-reduce.11.cloned.1.call-update) | async-done | bytes 2097168 | tf_op jit(solution)/shard_map/psum | solution.py:136
  406.7 6.2 %multiply_subtract_fusion.1 = (f32[4096,128]{1,0:T(8,128)}, f32[4096,128]{1,0:T(8,128)}) fusion(f32[4096,128]{1,0:T(8,128)} %get-tuple-element.19, f32[4096,128]{1,0:T(8,128)} %all-gather.5.cloned.1.call-done, f32[4096,128]{1,0:T(8,128)} %all-gather.7.cloned.1.call-done, f32[4096,128]{1,0:T(8,128)S(1)} %copy-done.3, f32[4096,128]{1,0:T(8,128)} %all-reduce.11.cloned.1.call-done), kind=kLoop, calls=%fused_computation.26 | loop fusion | flops 3670016 | bytes 14680064 | tf_op jit(solution)/shard_map/sub | solution.py:140
  412.9 2.2 gather_fusion.1
  415.1 0.1 broadcast_select_fusion.1
  415.2 8.5 %fusion.4 = f32[64,1,128]{2,1,0:T(1,128)S(1)} fusion(f32[64,128,1]{1,2,0:T(1,128)S(1)} %bitcast.131, f32[1,64,128,128]{3,2,1,0:T(8,128)} %param.15), kind=kOutput, calls=%fused_computation.16 | convolution fusion | flops 12582912 | bytes 4259840 | tf_op jit(solution)/shard_map/skij,skj->ski/dot_general | solution.py:29
  423.6 0.3 fusion.13
  423.9 0.2 fusion.62
  424.2 3.7 fusion.2
  427.8 2.3 scatter_custom_fusion.4
  430.1 0.0 all-reduce.13.cloned.1.call-update
  430.2 0.9 scatter_custom_fusion.5
  431.0 10.6 %all-reduce.3 = f32[1,32,128]{2,1,0:T(8,128)S(1)} all-reduce(f32[1,32,128]{2,1,0:T(8,128)S(1)} %bitcast.136), channel_id=4, replica_groups=mesh['grp'=2,'scen'=4,'blk'=2,'sub'=2] {'blk','sub'}, use_global_device_ids=true, to_apply=%region_11.12.clone | all-reduce | flops 4096 | bytes 32768
  441.6 0.6 multiply_subtract_fusion.3
  442.2 5.4 all_gather.27
  447.6 0.8 gather_fusion.5
  448.4 79.0 %all-reduce.13.cloned.1.call-done = f32[4096,128]{1,0:T(8,128)} async-done(((f32[4096,128]{1,0:T(8,128)}), f32[4096,128]{1,0:T(8,128)}) %all-reduce.13.cloned.1.call-update) | async-done | bytes 2097168 | tf_op jit(solution)/shard_map/psum | solution.py:136
  527.3 6.2 %multiply_subtract_fusion = (f32[4096,128]{1,0:T(8,128)}, f32[4096,128]{1,0:T(8,128)}) fusion(f32[4096,128]{1,0:T(8,128)} %get-tuple-element.14, f32[4096,128]{1,0:T(8,128)} %all-gather.5.cloned.1.call-done, f32[4096,128]{1,0:T(8,128)} %all-gather.7.cloned.1.call-done, f32[4096,128]{1,0:T(8,128)S(1)} %copy-done.3, f32[4096,128]{1,0:T(8,128)} %all-reduce.13.cloned.1.call-done), kind=kLoop, calls=%fused_computation.24 | loop fusion | flops 3670016 | bytes 14680064 | tf_op jit(solution)/shard_map/sub | solution.py:140
  533.5 2.2 gather_fusion.2
  535.7 0.1 broadcast_select_fusion
  535.8 8.3 %fusion = f32[64,1,128]{2,1,0:T(1,128)S(1)} fusion(f32[64,128,1]{1,2,0:T(1,128)S(1)} %bitcast.129, f32[1,64,128,128]{3,2,1,0:T(8,128)} %param.15), kind=kOutput, calls=%fused_computation.12 | convolution fusion | flops 12582912 | bytes 4259840 | tf_op jit(solution)/shard_map/skij,skj->ski/dot_general | solution.py:29
  544.1 1.6 multiply_reduce_fusion.2
  545.7 1.6 constant_dynamic-slice_fusion
  547.2 31.1 %all-reduce.4 = (f32[1]{0:T(128)}, f32[1]{0:T(128)}, f32[1]{0:T(128)}) all-reduce(f32[1]{0:T(128)} %bitcast.54, f32[1]{0:T(128)} %bitcast.53, f32[1]{0:T(128)} %bitcast.52), channel_id=1, replica_groups=mesh['grp'=2,'scen'=4,'blk'=2,'sub'=2] {'scen','blk','sub'}, use_global_device_ids=true, to_apply=%region_17.18 | all-reduce | flops 3 | bytes 24 | tf_op jit(solution)/shard_map/psum | solution.py:159
  578.3 2.5 fusion.82
  (34 shorter events, 0.2 us)
Async XLA Ops:
  7.2 28.7 %copy-start = (f32[24,8,128]{2,1,0:T(8,128)S(1)}, f32[24,8,128]{2,1,0:T(8,128)}, u32[]{:S(2)}) copy-start(f32[24,8,128]{2,1,0:T(8,128)} %param.20) | copy-start | bytes 294916
  7.2 110.7 %all-reduce.9.cloned.1.call-start = ((), (), s32[]{:S(2)}) async-start(), calls=%async_computation.4 | async-start | bytes 4194304 | tf_op jit(solution)/shard_map/psum | solution.py:136
  14.8 5.1 copy-start.9
  14.8 6.7 %copy-start.11 = (u32[32]{0:T(128)S(1)}, u32[32]{0:T(128)}, u32[]{:S(2)}) copy-start(u32[32]{0:T(128)} %constant.109) | copy-start | bytes 388
  14.8 21.3 %copy-start.4 = (f32[1,8,128]{2,1,0:T(8,128)S(1)}, f32[1,8,128]{2,1,0:T(8,128)}, u32[]{:S(2)}) copy-start(f32[1,8,128]{2,1,0:T(8,128)} %param.25) | copy-start | bytes 12292
  14.8 21.3 %copy-start.7 = (f32[1,8,128]{2,1,0:T(8,128)S(1)}, f32[1,8,128]{2,1,0:T(8,128)}, u32[]{:S(2)}) copy-start(f32[1,8,128]{2,1,0:T(8,128)} %param.28) | copy-start | bytes 12292
  14.8 21.3 %copy-start.8 = (f32[1,8,128]{2,1,0:T(8,128)S(1)}, f32[1,8,128]{2,1,0:T(8,128)}, u32[]{:S(2)}) copy-start(f32[1,8,128]{2,1,0:T(8,128)} %param.24) | copy-start | bytes 12292
  17.1 143.8 %all-gather.11.cloned.1.call-start = ((), (), s32[]{:S(2)}) async-start(), calls=%async_computation.3 | async-start | bytes 2228224 | tf_op jit(solution)/shard_map/all_gather | solution.py:112
  17.9 185.7 %all-gather.5.cloned.1.call-start = ((), (), s32[]{:S(2)}) async-start(), calls=%async_computation | async-start | bytes 2228224 | tf_op jit(solution)/shard_map/all_gather | solution.py:114
  18.6 227.4 %all-gather.7.cloned.1.call-start = ((), (), s32[]{:S(2)}) async-start(), calls=%async_computation.1 | async-start | bytes 2228224 | tf_op jit(solution)/shard_map/all_gather | solution.py:113
  19.2 269.3 %all-gather.9.cloned.1.call-start = ((), (), s32[]{:S(2)}) async-start(), calls=%async_computation.2 | async-start | bytes 2228224 | tf_op jit(solution)/shard_map/all_gather | solution.py:115
  19.8 386.9 %all-reduce.11.cloned.1.call-start = ((), (), s32[]{:S(2)}) async-start(), calls=%async_computation.5 | async-start | bytes 4194304 | tf_op jit(solution)/shard_map/psum | solution.py:136
  295.0 8.5 %copy-start.6 = (s32[1,64]{1,0:T(1,128)S(1)}, s32[1,64]{1,0:T(1,128)}, u32[]{:S(2)}) copy-start(s32[1,64]{1,0:T(1,128)} %param.16) | copy-start | bytes 772
  295.1 8.5 %copy-start.10 = (f32[1,8,128]{2,1,0:T(8,128)S(1)}, f32[1,8,128]{2,1,0:T(8,128)}, u32[]{:S(2)}) copy-start(f32[1,8,128]{2,1,0:T(8,128)} %param.26) | copy-start | bytes 12292
  295.1 8.8 %copy-start.5 = (f32[1,8,128]{2,1,0:T(8,128)S(1)}, f32[1,8,128]{2,1,0:T(8,128)}, u32[]{:S(2)}) copy-start(f32[1,8,128]{2,1,0:T(8,128)} %param.29) | copy-start | bytes 12292
  295.1 9.0 %copy-start.1 = (f32[1,64,128,128]{3,2,1,0:T(8,128)S(1)}, f32[1,64,128,128]{3,2,1,0:T(8,128)}, u32[]{:S(2)}) copy-start(f32[1,64,128,128]{3,2,1,0:T(8,128)} %param.15) | copy-start | bytes 12582916
  307.7 99.0 %copy-start.3 = (f32[4096,128]{1,0:T(8,128)S(1)}, f32[4096,128]{1,0:T(8,128)}, u32[]{:S(2)}) copy-start(f32[4096,128]{1,0:T(8,128)} %all-gather.11.cloned.1.call-done) | copy-start | bytes 6291460
  310.0 217.3 %all-reduce.13.cloned.1.call-start = ((), (), s32[]{:S(2)}) async-start(), calls=%async_computation.6 | async-start | bytes 4194304 | tf_op jit(solution)/shard_map/psum | solution.py:136
  415.2 9.0 %copy-start.2 = (f32[1,64,128,128]{3,2,1,0:T(8,128)S(1)}, f32[1,64,128,128]{3,2,1,0:T(8,128)}, u32[]{:S(2)}) copy-start(f32[1,64,128,128]{3,2,1,0:T(8,128)} %param.15) | copy-start | bytes 12582916
Sparse Core Ops, SparseCore 0:
  17.2 100.5 all-reduce.8
  120.3 40.6 all-gather.10
  163.3 40.1 all-gather.4
  205.8 40.1 all-gather.6
  248.2 40.1 all-gather.8
  310.2 96.5 all-reduce.10
  430.3 97.0 all-reduce.12
where the time goes:
time: 588 us
  waiting for transfers between devices  407 us (69%)
  blocking collectives  81.2 us (14%)
  matrix products  41.5 us (7%)
  other arithmetic  31.8 us (5%)
  between operations  16.3 us (3%)
  local copies, waits for them, and re-layouts  9.54 us (2%)
    psum x3, waiting for transfers between devices, shards(): grad_first = lax.psum(grad_first_part, ('scen', 'blk', 'sub'))  234 us
    all_gather x1, waiting for transfers between devices, shards(): lax.all_gather(cost_first, ('scen', 'blk', 'sub'), axis=0, tiled=True)  43.1 us
    all_gather x1, waiting for transfers between devices, shards(): lax.all_gather(upper_first, ('scen', 'blk', 'sub'), axis=0, tiled=True)  42.6 us
    all_gather x1, waiting for transfers between devices, shards(): lax.all_gather(lower_first, ('scen', 'blk', 'sub'), axis=0, tiled=True)  42.5 us
    all_gather x1, waiting for transfers between devices, shards(): lax.all_gather(first_start, ('scen', 'blk', 'sub'), axis=0, tiled=True)  42.4 us
    unnamed x3, blocking collectives  34.2 us
    psum x1, blocking collectives, shards(): squares.append(lax.psum(local_square, ('scen', 'blk', 'sub')))  31.1 us
    dot_general x3, matrix products, forward_window(): jnp.einsum('skij,skj->ski', block_matrices, blocks, precision=precise)  25.2 us
  transfers between devices with their start and end apart: 7, of which 7 were waited for; matrix products, arithmetic and copies ran while one was open for 1% of the time, Pallas kernels for 0%

commit v1 on v0

--- a/solution.py
+++ b/solution.py
@@ -133,7 +133,8 @@
         grad_second = lax.psum_scatter(
             grad_second_part, ("blk", "sub"), scatter_dimension=1, tiled=True
         )
-        grad_first = lax.psum(grad_first_part, ("scen", "blk", "sub"))
+        inner = lax.psum(grad_first_part, ("blk", "sub"))
+        grad_first = lax.psum(inner, "scen")
         first_next = jnp.clip(
             first_now - step_primal * (cost_all - grad_first), lower_all, upper_all
         )

time: 588 us -> 677 us (1.15)
  waiting for transfers between devices: 407 us -> 497 us
    psum x3 -> x6, waiting for transfers between devices: 234 us -> 375 us  [the longest x3 220 us: shards(): grad_first = lax.psum(inner, 'scen')]
    all_gather x1, waiting for transfers between devices: 43.1 us -> 0.01 us  [shards(): lax.all_gather(cost_first, ('scen', 'blk', 'sub'), axis=0, tiled=True)]
    all_gather x1, waiting for transfers between devices: 42.6 us -> 34.7 us  [shards(): lax.all_gather(upper_first, ('scen', 'blk', 'sub'), axis=0, tiled=True)]
  transfers between devices with their start and end apart: 7 -> 10, of which waited for: 7 -> 9; matrix products, arithmetic and copies ran while one was open for 1% -> 1% of each run, Pallas kernels for 0% -> 0%
where the time goes in v1:
time: 677 us
  waiting for transfers between devices  497 us (73%)
  blocking collectives  78.8 us (12%)
  matrix products  41.5 us (6%)
  other arithmetic  32 us (5%)
  between operations  18 us (3%)
  local copies, waits for them, and re-layouts  9.53 us (1%)
    psum x3, waiting for transfers between devices, shards(): grad_first = lax.psum(inner, 'scen')  220 us
    psum x3, waiting for transfers between devices, shards(): inner = lax.psum(grad_first_part, ('blk', 'sub'))  155 us
    all_gather x1, waiting for transfers between devices, shards(): lax.all_gather(first_start, ('scen', 'blk', 'sub'), axis=0, tiled=True)  42.3 us
    all_gather x1, waiting for transfers between devices, shards(): lax.all_gather(lower_first, ('scen', 'blk', 'sub'), axis=0, tiled=True)  42.2 us
    all_gather x1, waiting for transfers between devices, shards(): lax.all_gather(upper_first, ('scen', 'blk', 'sub'), axis=0, tiled=True)  34.7 us
    psum x1, blocking collectives, shards(): squares.append(lax.psum(local_square, ('scen', 'blk', 'sub')))  32.1 us
    unnamed x3, blocking collectives  30.9 us
    dot_general x3, matrix products, forward_window(): jnp.einsum('skij,skj->ski', block_matrices, blocks, precision=precise)  25.2 us
  transfers between devices with their start and end apart: 10, of which 9 were waited for; matrix products, arithmetic and copies ran while one was open for 1% of the time, Pallas kernels for 0%

profile of v1, /device:TPU:0, one launch (start us, length us, event | category | flops | bytes accessed | tf_op | source)
XLA Modules:
  0.0 676.7 jit_solution(16939191142630857177)
XLA Ops:
  8.7 0.7 fusion.79
  9.4 0.9 fusion.66
  10.3 5.3 fusion.10
  15.6 2.3 scatter_custom_fusion
  18.0 0.0 all-reduce.14.cloned.1.call-start
  18.0 54.2 %all-reduce.12.cloned.1.call-done = f32[4096,128]{1,0:T(8,128)} async-done(((f32[4096,128]{1,0:T(8,128)}), f32[4096,128]{1,0:T(8,128)}) %all-reduce.12.cloned.1.call-update) | async-done | bytes 2097168 | tf_op jit(solution)/shard_map/psum | solution.py:136
  72.2 0.0 all-gather.11.cloned.1.call-start
  72.3 0.5 all-gather.11.cloned.1.call-update
  72.8 0.0 all-gather.5.cloned.1.call-start
  72.8 0.5 all-gather.5.cloned.1.call-update
  73.4 0.0 all-gather.7.cloned.1.call-start
  73.4 0.5 all-gather.7.cloned.1.call-update
  74.0 0.0 all-gather.9.cloned.1.call-start
  74.0 0.7 all-gather.9.cloned.1.call-update
  74.7 0.0 all-reduce.16.cloned.1.call-start
  74.8 0.9 scatter_custom_fusion.1
  76.3 0.6 dynamic-slice
  77.6 10.5 %all-reduce.1 = f32[1,32,128]{2,1,0:T(8,128)S(1)} all-reduce(f32[1,32,128]{2,1,0:T(8,128)S(1)} %bitcast.135), channel_id=2, replica_groups=mesh['grp'=2,'scen'=4,'blk'=2,'sub'=2] {'blk','sub'}, use_global_device_ids=true, to_apply=%region_4.5.clone | all-reduce | flops 4096 | bytes 32768
  88.1 0.2 fusion.21
  88.3 5.2 all_gather.25
  93.5 0.8 gather_fusion.3
  94.3 77.4 %all-reduce.14.cloned.1.call-done = f32[4096,128]{1,0:T(8,128)} async-done(((f32[4096,128]{1,0:T(8,128)}), f32[4096,128]{1,0:T(8,128)}) %all-reduce.14.cloned.1.call-update) | async-done | bytes 2097168 | tf_op jit(solution)/shard_map/psum | solution.py:137
  171.8 34.7 %all-gather.5.cloned.1.call-done = f32[4096,128]{1,0:T(8,128)} async-done(((f32[256,128]{1,0:T(8,128)}), f32[4096,128]{1,0:T(8,128)}) %all-gather.5.cloned.1.call-update) | async-done | bytes 2097168 | tf_op jit(solution)/shard_map/all_gather | solution.py:114
  206.5 42.2 %all-gather.7.cloned.1.call-done = f32[4096,128]{1,0:T(8,128)} async-done(((f32[256,128]{1,0:T(8,128)}), f32[4096,128]{1,0:T(8,128)}) %all-gather.7.cloned.1.call-update) | async-done | bytes 2097168 | tf_op jit(solution)/shard_map/all_gather | solution.py:113
  248.7 42.3 %all-gather.9.cloned.1.call-done = f32[4096,128]{1,0:T(8,128)} async-done(((f32[256,128]{1,0:T(8,128)}), f32[4096,128]{1,0:T(8,128)}) %all-gather.9.cloned.1.call-update) | async-done | bytes 2097168 | tf_op jit(solution)/shard_map/all_gather | solution.py:115
  291.0 5.9 multiply_subtract_fusion.2
  296.9 0.6 gather_fusion
  297.5 0.1 broadcast_select_fusion.2
  297.6 8.5 %fusion.8 = f32[64,1,128]{2,1,0:T(1,128)S(1)} fusion(f32[64,128,1]{1,2,0:T(1,128)S(1)} %bitcast.130, f32[1,64,128,128]{3,2,1,0:T(8,128)} %param.15), kind=kOutput, calls=%fused_computation.20 | convolution fusion | flops 12582912 | bytes 4259840 | tf_op jit(solution)/shard_map/skij,skj->ski/dot_general | solution.py:29
  306.1 0.3 fusion.14
  306.4 0.2 fusion.64
  306.6 3.7 fusion.6
  310.3 2.4 scatter_custom_fusion.2
  312.7 0.0 all-reduce.18.cloned.1.call-start
  312.7 50.0 %all-reduce.16.cloned.1.call-done = f32[4096,128]{1,0:T(8,128)} async-done(((f32[4096,128]{1,0:T(8,128)}), f32[4096,128]{1,0:T(8,128)}) %all-reduce.16.cloned.1.call-update) | async-done | bytes 2097168 | tf_op jit(solution)/shard_map/psum | solution.py:136
  362.8 0.9 scatter_custom_fusion.3
  363.7 10.3 %all-reduce.2 = f32[1,32,128]{2,1,0:T(8,128)S(1)} all-reduce(f32[1,32,128]{2,1,0:T(8,128)S(1)} %bitcast.137), channel_id=3, replica_groups=mesh['grp'=2,'scen'=4,'blk'=2,'sub'=2] {'blk','sub'}, use_global_device_ids=true, to_apply=%region_9.10.clone | all-reduce | flops 4096 | bytes 32768
  374.0 5.2 all_gather.26
  379.2 0.8 gather_fusion.4
  380.0 71.7 %all-reduce.18.cloned.1.call-done = f32[4096,128]{1,0:T(8,128)} async-done(((f32[4096,128]{1,0:T(8,128)}), f32[4096,128]{1,0:T(8,128)}) %all-reduce.18.cloned.1.call-update) | async-done | bytes 2097168 | tf_op jit(solution)/shard_map/psum | solution.py:137
  451.7 6.2 multiply_subtract_fusion.1
  457.9 2.2 gather_fusion.1
  460.1 0.1 broadcast_select_fusion.1
  460.2 8.5 %fusion.4 = f32[64,1,128]{2,1,0:T(1,128)S(1)} fusion(f32[64,128,1]{1,2,0:T(1,128)S(1)} %bitcast.131, f32[1,64,128,128]{3,2,1,0:T(8,128)} %param.15), kind=kOutput, calls=%fused_computation.16 | convolution fusion | flops 12582912 | bytes 4259840 | tf_op jit(solution)/shard_map/skij,skj->ski/dot_general | solution.py:29
  468.6 0.3 fusion.13
  468.9 0.2 fusion.62
  469.1 3.7 fusion.2
  472.8 2.4 scatter_custom_fusion.4
  475.2 0.0 all-reduce.22.cloned.1.call-start
  475.2 50.4 %all-reduce.20.cloned.1.call-done = f32[4096,128]{1,0:T(8,128)} async-done(((f32[4096,128]{1,0:T(8,128)}), f32[4096,128]{1,0:T(8,128)}) %all-reduce.20.cloned.1.call-update) | async-done | bytes 2097168 | tf_op jit(solution)/shard_map/psum | solution.py:136
  525.7 0.9 scatter_custom_fusion.5
  526.6 10.1 %all-reduce.3 = f32[1,32,128]{2,1,0:T(8,128)S(1)} all-reduce(f32[1,32,128]{2,1,0:T(8,128)S(1)} %bitcast.136), channel_id=4, replica_groups=mesh['grp'=2,'scen'=4,'blk'=2,'sub'=2] {'blk','sub'}, use_global_device_ids=true, to_apply=%region_14.15.clone | all-reduce | flops 4096 | bytes 32768
  536.7 0.6 multiply_subtract_fusion.3
  537.3 5.4 all_gather.27
  542.7 0.8 gather_fusion.5
  543.5 71.2 %all-reduce.22.cloned.1.call-done = f32[4096,128]{1,0:T(8,128)} async-done(((f32[4096,128]{1,0:T(8,128)}), f32[4096,128]{1,0:T(8,128)}) %all-reduce.22.cloned.1.call-update) | async-done | bytes 2097168 | tf_op jit(solution)/shard_map/psum | solution.py:137
  614.6 6.2 multiply_subtract_fusion
  620.8 2.2 gather_fusion.2
  623.0 0.1 broadcast_select_fusion
  623.1 8.3 %fusion = f32[64,1,128]{2,1,0:T(1,128)S(1)} fusion(f32[64,128,1]{1,2,0:T(1,128)S(1)} %bitcast.129, f32[1,64,128,128]{3,2,1,0:T(8,128)} %param.15), kind=kOutput, calls=%fused_computation.12 | convolution fusion | flops 12582912 | bytes 4259840 | tf_op jit(solution)/shard_map/skij,skj->ski/dot_general | solution.py:29
  631.4 1.6 multiply_reduce_fusion.2
  633.0 1.6 constant_dynamic-slice_fusion
  634.5 32.1 %all-reduce.4 = (f32[1]{0:T(128)}, f32[1]{0:T(128)}, f32[1]{0:T(128)}) all-reduce(f32[1]{0:T(128)} %bitcast.54, f32[1]{0:T(128)} %bitcast.53, f32[1]{0:T(128)} %bitcast.52), channel_id=1, replica_groups=mesh['grp'=2,'scen'=4,'blk'=2,'sub'=2] {'scen','blk','sub'}, use_global_device_ids=true, to_apply=%region_20.21 | all-reduce | flops 3 | bytes 24 | tf_op jit(solution)/shard_map/psum | solution.py:160
  666.6 2.5 fusion.82
  (43 shorter events, 0.3 us)
Async XLA Ops:
  8.0 80.1 %copy-start = (f32[24,8,128]{2,1,0:T(8,128)S(1)}, f32[24,8,128]{2,1,0:T(8,128)}, u32[]{:S(2)}) copy-start(f32[24,8,128]{2,1,0:T(8,128)} %param.20) | copy-start | bytes 294916
  8.0 64.2 %all-reduce.12.cloned.1.call-start = ((), (), s32[]{:S(2)}) async-start(), calls=%async_computation.4 | async-start | bytes 4194304 | tf_op jit(solution)/shard_map/psum | solution.py:136
  17.9 56.8 %copy-start.9 = (s32[1,64]{1,0:T(1,128)S(1)}, s32[1,64]{1,0:T(1,128)}, u32[]{:S(2)}) copy-start(s32[1,64]{1,0:T(1,128)} %param.17) | copy-start | bytes 772
  17.9 58.4 %copy-start.11 = (u32[32]{0:T(128)S(1)}, u32[32]{0:T(128)}, u32[]{:S(2)}) copy-start(u32[32]{0:T(128)} %constant.109) | copy-start | bytes 388
  17.9 70.4 %copy-start.4 = (f32[1,8,128]{2,1,0:T(8,128)S(1)}, f32[1,8,128]{2,1,0:T(8,128)}, u32[]{:S(2)}) copy-start(f32[1,8,128]{2,1,0:T(8,128)} %param.25) | copy-start | bytes 12292
  17.9 70.4 %copy-start.7 = (f32[1,8,128]{2,1,0:T(8,128)S(1)}, f32[1,8,128]{2,1,0:T(8,128)}, u32[]{:S(2)}) copy-start(f32[1,8,128]{2,1,0:T(8,128)} %param.28) | copy-start | bytes 12292
  17.9 70.4 %copy-start.8 = (f32[1,8,128]{2,1,0:T(8,128)S(1)}, f32[1,8,128]{2,1,0:T(8,128)}, u32[]{:S(2)}) copy-start(f32[1,8,128]{2,1,0:T(8,128)} %param.24) | copy-start | bytes 12292
  18.0 153.8 %all-reduce.14.cloned.1.call-start = ((), (), s32[]{:S(2)}) async-start(), calls=%async_computation.5 | async-start | bytes 4194304 | tf_op jit(solution)/shard_map/psum | solution.py:137
  72.2 99.6 %all-gather.11.cloned.1.call-start = ((), (), s32[]{:S(2)}) async-start(), calls=%async_computation.3 | async-start | bytes 2228224 | tf_op jit(solution)/shard_map/all_gather | solution.py:112
  72.8 133.7 %all-gather.5.cloned.1.call-start = ((), (), s32[]{:S(2)}) async-start(), calls=%async_computation | async-start | bytes 2228224 | tf_op jit(solution)/shard_map/all_gather | solution.py:114
  73.4 175.3 %all-gather.7.cloned.1.call-start = ((), (), s32[]{:S(2)}) async-start(), calls=%async_computation.1 | async-start | bytes 2228224 | tf_op jit(solution)/shard_map/all_gather | solution.py:113
  74.0 217.0 %all-gather.9.cloned.1.call-start = ((), (), s32[]{:S(2)}) async-start(), calls=%async_computation.2 | async-start | bytes 2228224 | tf_op jit(solution)/shard_map/all_gather | solution.py:115
  74.7 288.0 %all-reduce.16.cloned.1.call-start = ((), (), s32[]{:S(2)}) async-start(), calls=%async_computation.6 | async-start | bytes 4194304 | tf_op jit(solution)/shard_map/psum | solution.py:136
  297.6 8.5 %copy-start.6 = (s32[1,64]{1,0:T(1,128)S(1)}, s32[1,64]{1,0:T(1,128)}, u32[]{:S(2)}) copy-start(s32[1,64]{1,0:T(1,128)} %param.16) | copy-start | bytes 772
  297.6 8.5 %copy-start.10 = (f32[1,8,128]{2,1,0:T(8,128)S(1)}, f32[1,8,128]{2,1,0:T(8,128)}, u32[]{:S(2)}) copy-start(f32[1,8,128]{2,1,0:T(8,128)} %param.26) | copy-start | bytes 12292
  297.6 8.8 %copy-start.5 = (f32[1,8,128]{2,1,0:T(8,128)S(1)}, f32[1,8,128]{2,1,0:T(8,128)}, u32[]{:S(2)}) copy-start(f32[1,8,128]{2,1,0:T(8,128)} %param.29) | copy-start | bytes 12292
  297.6 9.0 %copy-start.1 = (f32[1,64,128,128]{3,2,1,0:T(8,128)S(1)}, f32[1,64,128,128]{3,2,1,0:T(8,128)}, u32[]{:S(2)}) copy-start(f32[1,64,128,128]{3,2,1,0:T(8,128)} %param.15) | copy-start | bytes 12582916
  312.6 139.1 %copy-start.3 = (f32[4096,128]{1,0:T(8,128)S(1)}, f32[4096,128]{1,0:T(8,128)}, u32[]{:S(2)}) copy-start(f32[4096,128]{1,0:T(8,128)} %all-gather.11.cloned.1.call-done) | copy-start | bytes 6291460
  312.7 139.0 %all-reduce.18.cloned.1.call-start = ((), (), s32[]{:S(2)}) async-start(), calls=%async_computation.7 | async-start | bytes 4194304 | tf_op jit(solution)/shard_map/psum | solution.py:137
  362.8 162.9 %all-reduce.20.cloned.1.call-start = ((), (), s32[]{:S(2)}) async-start(), calls=%async_computation.8 | async-start | bytes 4194304 | tf_op jit(solution)/shard_map/psum | solution.py:136
  460.1 9.0 %copy-start.2 = (f32[1,64,128,128]{3,2,1,0:T(8,128)S(1)}, f32[1,64,128,128]{3,2,1,0:T(8,128)}, u32[]{:S(2)}) copy-start(f32[1,64,128,128]{3,2,1,0:T(8,128)} %param.15) | copy-start | bytes 12582916
  475.2 139.4 %all-reduce.22.cloned.1.call-start = ((), (), s32[]{:S(2)}) async-start(), calls=%async_computation.9 | async-start | bytes 4194304 | tf_op jit(solution)/shard_map/psum | solution.py:137
Sparse Core Ops, SparseCore 0:
  18.1 54.0 all-reduce.11
  74.7 97.0 all-reduce.13
  312.8 49.9 all-reduce.15
  365.1 86.5 all-reduce.17
  475.3 50.3 all-reduce.19
  528.0 86.5 all-reduce.21
Sparse Core Ops, SparseCore 1:
  74.8 88.6 all-gather.10
  165.5 40.9 all-gather.4
  208.5 40.1 all-gather.6
  250.9 40.1 all-gather.8
